TPU v7x, 512 devices: a whole 4x8x8 slice. The times are simulated.
512 devices in a mesh: ctx: 32 (over y, z_lo), ep: 16 (over z_hi, x, core).
Axes of the slice: x: 4, y: 8, z: 8 (z_hi: 2, z_lo: 4; z = z_hi * 4 + z_lo), core: 2. Of those that a mesh axis runs over, the one named last changes fastest.
Arguments:
- queries: bfloat16 [16, 4096, 2048], P('ep', 'ctx'), may hold values from -100 to 100
- keys: bfloat16 [16, 4096, 2048], P('ep', 'ctx'), may hold values from -4 to 4
- values: bfloat16 [16, 4096, 2048], P('ep', 'ctx'), may hold values from -6 to 6
- doc_ids: int32 [16, 4096], P('ep', 'ctx'), may hold values from 0 to 31, never falling along the last dimension, each value on 1 to 256 neighbouring positions
- routes: int32 [16, 4096, 1], P('ep', 'ctx'), may hold values from 0 to 63
- route_weight: float32 [16, 4096, 1], P('ep', 'ctx'), may hold values from 0.2 to 1
- norm_gain: float32 [2048], replicated, may hold values from 0.25 to 1.75
- w_gate: bfloat16 [2048, 90112], P(None, ('ctx', 'ep')), may hold values from -0.125 to 0.125
- w_up: bfloat16 [2048, 90112], P(None, ('ctx', 'ep')), may hold values from -0.125 to 0.125
- w_down: bfloat16 [90112, 2048], P(('ctx', 'ep')), may hold values from -0.15625 to 0.15625
- grad_out: bfloat16 [16, 4096, 2048], P('ep', 'ctx'), may hold values from -6 to 6
Outputs:
- grad_in: bfloat16 [16, 4096, 2048], P('ep', 'ctx')
Inputs may be any that keep to these rules, and one draw needn't show every extreme that they name: `doc_ids`: no document has more than 256 tokens; ids never fall along a sequence.
All inputs are finite; a program needn't handle non-finite values.
Results may differ from a plain program's by a relative error of at most 0.0086.
Values may be sent and summed in bfloat16 or wider, within the bound.
A program may use at most 64 MiB of HBM per device.

v0:
```python
import math

import jax
import jax.numpy as jnp
from jax import lax
from jax.sharding import PartitionSpec as P

HEADS = 16
HEAD = 128
EXPERTS = 64
FF = 1408
CAP = 2
REACH = 2


def shifted(value, axis, steps):
    count = lax.axis_size(axis)
    leading, last = (max(0, -steps), min(count, count - steps))
    return lax.ppermute(value, axis, [(source, source + steps) for source in range(leading, last)])


def expert_piece(operands, gate_piece, up_piece, down_piece):
    normed_in, grads_in = operands
    gate_pre = jnp.einsum(
        "aeqkd,dqw->aeqkw", normed_in, gate_piece, preferred_element_type=jnp.float32
    )
    up_pre = jnp.einsum("aeqkd,dqw->aeqkw", normed_in, up_piece, preferred_element_type=jnp.float32)
    grad_act = jnp.einsum(
        "aeqkd,qwd->aeqkw", grads_in, down_piece, preferred_element_type=jnp.float32
    )
    sigmoid_gate = jax.nn.sigmoid(gate_pre)
    gate_act = gate_pre * sigmoid_gate
    act_slope = sigmoid_gate * (1.0 + gate_pre * (1.0 - sigmoid_gate))
    grad_gate = (grad_act * up_pre * act_slope).astype(jnp.bfloat16)
    grad_up = (grad_act * gate_act).astype(jnp.bfloat16)
    partial_rows = jnp.einsum(
        "aeqkw,dqw->aeqkd", grad_gate, gate_piece, preferred_element_type=jnp.float32
    )
    partial_rows = partial_rows + jnp.einsum(
        "aeqkw,dqw->aeqkd", grad_up, up_piece, preferred_element_type=jnp.float32
    )
    return partial_rows.astype(jnp.bfloat16)


def shards(
    queries, keys, values, doc_ids, routes, route_weight, norm_gain, w_gate, w_up, w_down, grad_out
):
    stretch_rows = queries.shape[1]
    model_width = queries.shape[2]
    ctx_count = lax.axis_size("ctx")
    ep_count = lax.axis_size("ep")
    doc_tags = doc_ids[0] + 1
    packed = jnp.stack([keys[0], values[0]])
    key_blocks = [packed]
    tag_blocks = [doc_tags]
    current_keys = packed
    current_tags = doc_tags
    for distance in range(REACH):
        current_keys, current_tags = shifted((current_keys, current_tags), "ctx", 1)
        key_blocks.append(current_keys)
        tag_blocks.append(current_tags)
    key_values = jnp.concatenate(key_blocks, axis=1)
    all_tags = jnp.concatenate(tag_blocks)
    query_heads = queries[0].reshape(stretch_rows, HEADS, HEAD)
    key_heads = key_values[0].reshape(-1, HEADS, HEAD)
    value_heads = key_values[1].reshape(-1, HEADS, HEAD)
    scores = jnp.einsum(
        "qhd,khd->hqk", query_heads, key_heads, preferred_element_type=jnp.float32
    ) * (1.0 / math.sqrt(HEAD))
    query_pos = jnp.arange(stretch_rows)[:, None]
    key_pos = jnp.arange(key_values.shape[1])[None, :]
    visible = (doc_tags[:, None] == all_tags[None, :]) & (
        (key_pos >= stretch_rows) | (key_pos <= query_pos)
    )
    scores = jnp.where(visible[None], scores, -1e30)
    row_max = jnp.max(scores, axis=-1, keepdims=True)
    weights_exp = jnp.exp(scores - row_max)
    probs = (weights_exp / jnp.sum(weights_exp, axis=-1, keepdims=True)).astype(jnp.bfloat16)
    attended = jnp.einsum("hqk,khd->qhd", probs, value_heads, preferred_element_type=jnp.float32)
    hidden_bf = attended.reshape(stretch_rows, model_width).astype(jnp.bfloat16)
    hidden = lax.optimization_barrier(hidden_bf).astype(jnp.float32)
    inv_rms = lax.rsqrt(jnp.mean(hidden * hidden, axis=-1, keepdims=True) + 1e-06)
    normed = (hidden * inv_rms * norm_gain).astype(jnp.bfloat16)
    grad_f = grad_out[0].astype(jnp.float32)
    grad_rows = (route_weight[0, :, 0:1] * grad_f).astype(jnp.bfloat16)
    expert_ids = routes[0, :, 0]
    onehot = (expert_ids[:, None] == jnp.arange(EXPERTS, dtype=jnp.int32)[None, :]).astype(
        jnp.int32
    )
    running = jnp.cumsum(onehot, axis=0)
    slot_rank = jnp.sum(onehot * (running - 1), axis=1)
    row_target = jnp.where(slot_rank < CAP, expert_ids * CAP + slot_rank, -1)
    selector = (jnp.arange(EXPERTS * CAP, dtype=jnp.int32)[:, None] == row_target[None, :]).astype(
        jnp.bfloat16
    )
    groups = EXPERTS // ctx_count
    normed_slots = (
        jnp.dot(selector, normed, preferred_element_type=jnp.float32)
        .astype(jnp.bfloat16)
        .reshape(ctx_count, groups, CAP, model_width)
    )
    grad_slots = (
        jnp.dot(selector, grad_rows, preferred_element_type=jnp.float32)
        .astype(jnp.bfloat16)
        .reshape(ctx_count, groups, CAP, model_width)
    )
    piece_cols = w_gate.shape[1]
    local_experts = max(1, piece_cols // FF)
    span_cols = min(piece_cols, FF)
    per_expert = ep_count * local_experts // groups
    gate_piece = w_gate.reshape(model_width, local_experts, span_cols)
    up_piece = w_up.reshape(model_width, local_experts, span_cols)
    down_piece = w_down.reshape(local_experts, span_cols, model_width)

    def spread_copies(slots):
        copies = jnp.broadcast_to(
            slots[:, :, None], (slots.shape[0], groups, per_expert, CAP, model_width)
        )
        return copies.reshape(slots.shape[0], ep_count, local_experts, CAP, model_width)

    owner_normed, owner_grads = (
        lax.all_to_all(normed_slots, "ctx", split_axis=0, concat_axis=0, tiled=True),
        lax.all_to_all(grad_slots, "ctx", split_axis=0, concat_axis=0, tiled=True),
    )
    partials = expert_piece(
        (
            lax.all_to_all(
                spread_copies(owner_normed), "ep", split_axis=1, concat_axis=1, tiled=True
            ),
            lax.all_to_all(
                spread_copies(owner_grads), "ep", split_axis=1, concat_axis=1, tiled=True
            ),
        ),
        gate_piece,
        up_piece,
        down_piece,
    )
    returned = lax.all_to_all(partials, "ep", split_axis=1, concat_axis=1, tiled=True)
    summed = jnp.sum(
        returned.reshape(ctx_count, groups, per_expert, CAP, model_width).astype(jnp.float32),
        axis=2,
    ).astype(jnp.bfloat16)
    combined = lax.all_to_all(summed, "ctx", split_axis=0, concat_axis=0, tiled=True).reshape(
        EXPERTS * CAP, model_width
    )
    grad_normed = jnp.einsum("rt,rd->td", selector, combined, preferred_element_type=jnp.float32)
    gained = grad_normed * norm_gain
    grad_in = (
        grad_f
        + inv_rms * gained
        - hidden * inv_rms * inv_rms * inv_rms * jnp.mean(hidden * gained, axis=-1, keepdims=True)
    )
    return grad_in.astype(jnp.bfloat16)[None]


def solution(mesh):
    in_specs = (
        P("ep", "ctx", None),
        P("ep", "ctx", None),
        P("ep", "ctx", None),
        P("ep", "ctx"),
        P("ep", "ctx", None),
        P("ep", "ctx", None),
        P(),
        P(None, ("ctx", "ep")),
        P(None, ("ctx", "ep")),
        P(("ctx", "ep"), None),
        P("ep", "ctx", None),
    )
    out_specs = P("ep", "ctx", None)
    return jax.shard_map(shards, mesh=mesh, in_specs=in_specs, out_specs=out_specs, check_vma=False)
```

profile of v0, /device:TPU:8, one launch (start us, length us, event | category | flops | bytes accessed | tf_op | source)
XLA Modules:
  0.0 505.3 jit_solution(9709923083660228643)
XLA Ops:
  0.0 1.4 copy.38
  1.4 1.3 copy.39
  2.8 0.1 pad_maximum_fusion.1
  2.9 4.3 collective-permute-start
  7.2 4.3 collective-permute-start.2
  11.5 22.4 %collective-permute-done = bf16[2,128,2048]{1,2,0:T(8,128)(2,1)} collective-permute-done((bf16[2,128,2048]{1,2,0:T(8,128)(2,1)S(1)}, bf16[2,128,2048]{1,2,0:T(8,128)(2,1)}, u32[]{:S(2)}, u32[]{:S(2)}) %collective-permute-start) | collective-permute-done | bytes 1048608 | tf_op jit(solution)/shard_map/ppermute | solution.py:19
  33.9 1.9 collective-permute-start.1
  35.9 0.2 reduce_window_sum.11
  36.1 0.2 select_reduce_fusion
  36.3 0.4 convolution_convert_fusion.1
  36.7 1.1 reshape.152
  37.8 12.0 %all-to-all-start = ((bf16[32,2,2,2048]{3,2,1,0:T(2,128)(2,1)}), bf16[32,2,2,2048]{3,2,1,0:T(2,128)(2,1)S(1)}, u32[]{:S(2)}, u32[]{:S(2)}) async-start(bf16[32,2,2,2048]{3,2,1,0:T(2,128)(2,1)} %reshape.152), calls=%async_computation | async-start | bytes 1048576 | tf_op jit(solution)/shard_map/all_to_all | solution.py:123
  49.8 3.4 collective-permute-start.3
  53.2 1.1 copy.57
  54.4 23.6 %collective-permute-done.3 = s32[128]{0:T(128)S(1)} collective-permute-done((s32[128]{0:T(128)S(1)}, s32[128]{0:T(128)S(1)}, u32[]{:S(2)}, u32[]{:S(2)}) %collective-permute-start.3) | collective-permute-done | bytes 544 | tf_op jit(solution)/shard_map/ppermute | solution.py:19
  77.9 0.2 fusion.73
  78.1 1.8 pad_maximum_fusion
  79.9 0.3 fusion.82
  80.2 0.6 fusion.66
  80.9 1.0 fusion.83
  81.8 0.6 fusion.34
  82.4 0.2 copy.43
  82.6 0.2 fusion.49
  82.8 0.4 convolution_convert_fusion
  83.2 1.1 reshape.155
  84.4 12.7 %all-to-all-start.2 = ((bf16[32,2,2,2048]{3,2,1,0:T(2,128)(2,1)}), bf16[32,2,2,2048]{3,2,1,0:T(2,128)(2,1)}, u32[]{:S(2)}, u32[]{:S(2)}) async-start(bf16[32,2,2,2048]{3,2,1,0:T(2,128)(2,1)} %reshape.155), calls=%async_computation.2 | async-start | bytes 1048576 | tf_op jit(solution)/shard_map/all_to_all | solution.py:122
  97.0 0.4 copy.44
  97.4 13.2 %all-to-all-done.2 = bf16[32,2,2,2048]{3,2,1,0:T(2,128)(2,1)} async-done(((bf16[32,2,2,2048]{3,2,1,0:T(2,128)(2,1)}), bf16[32,2,2,2048]{3,2,1,0:T(2,128)(2,1)}, u32[]{:S(2)}, u32[]{:S(2)}) %all-to-all-start.2) | async-done | bytes 524320 | tf_op jit(solution)/shard_map/all_to_all | solution.py:122
  110.6 5.5 %broadcast_in_dim.25 = bf16[32,2,8,2,2048]{4,3,0,2,1:T(2,128)(2,1)} broadcast(bf16[32,2,2,2048]{3,2,0,1:T(2,128)(2,1)S(1)} %copy.44), dimensions={0,1,3,4} | broadcast | bytes 4718592 | tf_op jit(solution)/shard_map/broadcast_in_dim | solution.py:116
  116.1 14.7 %all-to-all-start.1 = ((bf16[32,16,1,2,2048]{4,3,0,2,1:T(2,128)(2,1)}), bf16[32,16,1,2,2048]{4,3,0,2,1:T(2,128)(2,1)}, u32[]{:S(2)}, u32[]{:S(2)}) async-start(bf16[32,16,1,2,2048]{4,3,0,2,1:T(2,128)(2,1)} %bitcast.126), calls=%async_computation.1 | async-start | bytes 8388608 | tf_op jit(solution)/shard_map/all_to_all | solution.py:130
  130.8 1.4 copy.46
  132.2 97.0 %all-to-all-done.1 = bf16[32,16,1,2,2048]{4,3,0,2,1:T(2,128)(2,1)} async-done(((bf16[32,16,1,2,2048]{4,3,0,2,1:T(2,128)(2,1)}), bf16[32,16,1,2,2048]{4,3,0,2,1:T(2,128)(2,1)}, u32[]{:S(2)}, u32[]{:S(2)}) %all-to-all-start.1) | async-done | bytes 4194336 | tf_op jit(solution)/shard_map/all_to_all | solution.py:130
  229.2 5.5 %broadcast_in_dim.26 = bf16[32,2,8,2,2048]{4,3,0,2,1:T(2,128)(2,1)} broadcast(bf16[32,2,2,2048]{3,2,0,1:T(2,128)(2,1)S(1)} %copy.46), dimensions={0,1,3,4} | broadcast | bytes 4718592 | tf_op jit(solution)/shard_map/broadcast_in_dim | solution.py:116
  234.7 4.7 all-to-all-start.3
  239.4 5.7 %fusion.16 = f32[32,16,1,2,176]{4,1,3,0,2:T(8,128)} fusion(bf16[32,16,1,2,2048]{4,3,0,2,1:T(2,128)(2,1)} %all-to-all-done.1, bf16[176,2048]{1,0:T(8,128)(2,1)S(1)} %copy-done.5), kind=kOutput, calls=%fused_computation.28 | convolution fusion | flops 738197504 | bytes 5636096 | tf_op jit(solution)/shard_map/aeqkd,qwd->aeqkw/dot_general | solution.py:28
  245.1 49.3 %all-to-all-done.3 = bf16[32,16,1,2,2048]{4,3,0,2,1:T(2,128)(2,1)} async-done(((bf16[32,16,1,2,2048]{4,3,0,2,1:T(2,128)(2,1)}), bf16[32,16,1,2,2048]{4,3,0,2,1:T(2,128)(2,1)}, u32[]{:S(2)}, u32[]{:S(2)}) %all-to-all-start.3) | async-done | bytes 4194336 | tf_op jit(solution)/shard_map/all_to_all | solution.py:127
  294.4 5.8 %fusion.22 = f32[32,16,1,2,176]{4,1,3,0,2:T(8,128)} fusion(bf16[32,16,1,2,2048]{4,3,0,2,1:T(2,128)(2,1)} %all-to-all-done.3, bf16[2048,176]{0,1:T(8,128)(2,1)} %param.18), kind=kOutput, calls=%fused_computation.30 | convolution fusion | flops 738197504 | bytes 5636096 | tf_op jit(solution)/shard_map/aeqkd,dqw->aeqkw/dot_general | solution.py:24
  300.2 10.7 %fusion.41 = f32[32,16,2,2048]{3,1,2,0:T(8,128)} fusion(f32[32,16,1,2,176]{4,1,3,0,2:T(8,128)} %fusion.16, bf16[32,16,1,2,2048]{4,3,0,2,1:T(2,128)(2,1)} %all-to-all-done.3, f32[32,16,1,2,176]{4,1,3,0,2:T(8,128)} %fusion.22, bf16[2048,176]{0,1:T(8,128)(2,1)S(1)} %copy-done.6, bf16[2048,176]{0,1:T(8,128)(2,1)S(1)} %copy-done), kind=kOutput, calls=%fused_computation.40 | convolution fusion | flops 1478197248 | bytes 15466496 | tf_op jit(solution)/shard_map/aeqkw,dqw->aeqkd/dot_general | solution.py:36
  310.8 7.3 %fusion.10 = bf16[32,16,1,2,2048]{4,1,3,0,2:T(8,128)(2,1)} fusion(f32[32,16,2,2048]{3,1,2,0:T(8,128)} %fusion.41, bf16[2048,176]{0,1:T(8,128)(2,1)S(1)} %copy-done, f32[32,16,1,2,176]{4,1,3,0,2:T(8,128)} %fusion.16, f32[32,16,1,2,176]{4,1,3,0,2:T(8,128)} %fusion.22), kind=kOutput, calls=%fused_computation.12 | convolution fusion | flops 743473152 | bytes 14745600 | tf_op jit(solution)/shard_map/aeqkw,dqw->aeqkd/dot_general | solution.py:39
  318.1 6.7 %copy.48 = bf16[32,16,1,2,2048]{4,3,0,2,1:T(2,128)(2,1)S(1)} copy(bf16[32,16,1,2,2048]{4,1,3,0,2:T(8,128)(2,1)} %fusion.10) | data formatting | bytes 8388608 | tf_op jit(solution)/shard_map/convert_element_type | solution.py:42
  324.9 64.9 %all_to_all.30 = bf16[32,16,1,2,2048]{4,3,0,2,1:T(2,128)(2,1)} all-to-all(bf16[32,16,1,2,2048]{4,3,0,2,1:T(2,128)(2,1)S(1)} %copy.48), channel_id=1, replica_groups=mesh['ctx'=32,'ep'=16] {'ep'}, dimensions={1} | all-to-all | bytes 8388608 | tf_op jit(solution)/shard_map/all_to_all | solution.py:138
  389.8 6.3 %bitcast_reduce_fusion = bf16[32,2,2,2048]{3,2,0,1:T(2,128)(2,1)S(1)} fusion(bf16[32,2,8,2,2048]{4,3,0,2,1:T(2,128)(2,1)} %bitcast.128), kind=kLoop, calls=%fused_computation.2 | loop fusion | flops 1835008 | bytes 4718592 | tf_op jit(solution)/shard_map/reduce_sum | solution.py:139
  396.1 0.5 copy.56
  396.7 106.2 %all_to_all.31 = bf16[32,2,2,2048]{3,1,2,0:T(2,128)(2,1)S(1)} all-to-all(bf16[32,2,2,2048]{3,1,2,0:T(2,128)(2,1)S(1)} %copy.56), channel_id=1, replica_groups=mesh['ctx'=32,'ep'=16] {'ctx'}, dimensions={0} | all-to-all | bytes 1048576 | tf_op jit(solution)/shard_map/all_to_all | solution.py:143
  502.9 0.5 copy.50
  503.4 0.2 reshape.161
  503.6 0.4 fusion.50
  504.1 1.2 fusion.62
  (26 shorter events, 0.2 us)
Async XLA Ops:
  0.0 300.2 %copy-start = (bf16[2048,176]{0,1:T(8,128)(2,1)S(1)}, bf16[2048,176]{0,1:T(8,128)(2,1)}, u32[]{:S(2)}) copy-start(bf16[2048,176]{0,1:T(8,128)(2,1)} %param.19) | copy-start | bytes 2162692
  0.0 7.2 %copy-start.7 = (s32[1,128]{1,0:T(1,128)S(1)}, s32[1,128]{1,0:T(1,128)}, u32[]{:S(2)}) copy-start(s32[1,128]{1,0:T(1,128)} %param.14) | copy-start | bytes 1540
  0.0 35.8 %copy-start.3 = (s32[1,128,1]{1,2,0:T(1,128)S(1)}, s32[1,128,1]{1,2,0:T(1,128)}, u32[]{:S(2)}) copy-start(s32[1,128,1]{1,2,0:T(1,128)} %param.15) | copy-start | bytes 1540
  0.0 36.3 %copy-start.1 = (bf16[1,128,2048]{2,1,0:T(8,128)(2,1)S(1)}, bf16[1,128,2048]{2,1,0:T(8,128)(2,1)}, u32[]{:S(2)}) copy-start(bf16[1,128,2048]{2,1,0:T(8,128)(2,1)} %param.21) | copy-start | bytes 1572868
  0.0 36.3 %copy-start.4 = (f32[1,128,1]{1,2,0:T(1,128)S(1)}, f32[1,128,1]{1,2,0:T(1,128)}, u32[]{:S(2)}) copy-start(f32[1,128,1]{1,2,0:T(1,128)} %param.16) | copy-start | bytes 1540
  2.9 31.0 %collective-permute-start = (bf16[2,128,2048]{1,2,0:T(8,128)(2,1)S(1)}, bf16[2,128,2048]{1,2,0:T(8,128)(2,1)}, u32[]{:S(2)}, u32[]{:S(2)}) collective-permute-start(bf16[2,128,2048]{1,2,0:T(8,128)(2,1)S(1)} %pad_maximum_fusion.1), channel_id=1, source_target_pairs={{0,16},{16,32},{32,48},{48,64},{64,80},{80,96},{96,112},{112,128},... | collective-permute-start | bytes 3145736 | tf_op jit(solution)/shard_map/ppermute | solution.py:19
  7.2 42.6 %collective-permute-start.2 = (s32[128]{0:T(128)S(1)}, s32[128]{0:T(128)S(1)}, u32[]{:S(2)}, u32[]{:S(2)}) collective-permute-start(s32[128]{0:T(128)S(1)} %add_bitcast_fusion), channel_id=1, source_target_pairs={{0,16},{16,32},{32,48},{48,64},{64,80},{80,96},{96,112},{112,128},... | collective-permute-start | bytes 1544 | tf_op jit(solution)/shard_map/ppermute | solution.py:19
  33.9 44.2 %collective-permute-start.1 = (bf16[2,128,2048]{1,2,0:T(8,128)(2,1)}, bf16[2,128,2048]{1,2,0:T(8,128)(2,1)}, u32[]{:S(2)}, u32[]{:S(2)}) collective-permute-start(bf16[2,128,2048]{1,2,0:T(8,128)(2,1)} %collective-permute-done), channel_id=1, source_target_pairs={{0,16},{16,32},{32,48},{48,64},{64,80},{80,96},{96,112},{112,128},... | collective-permute-start | bytes 3145736 | tf_op jit(solution)/shard_map/ppermute | solution.py:19
  37.8 46.5 %all-to-all-start = ((bf16[32,2,2,2048]{3,2,1,0:T(2,128)(2,1)}), bf16[32,2,2,2048]{3,2,1,0:T(2,128)(2,1)S(1)}, u32[]{:S(2)}, u32[]{:S(2)}) async-start(bf16[32,2,2,2048]{3,2,1,0:T(2,128)(2,1)} %reshape.152), calls=%async_computation | async-start | bytes 1048576 | tf_op jit(solution)/shard_map/all_to_all | solution.py:123
  49.8 28.1 %collective-permute-start.3 = (s32[128]{0:T(128)S(1)}, s32[128]{0:T(128)S(1)}, u32[]{:S(2)}, u32[]{:S(2)}) collective-permute-start(s32[128]{0:T(128)S(1)} %collective-permute-done.2), channel_id=1, source_target_pairs={{0,16},{16,32},{32,48},{48,64},{64,80},{80,96},{96,112},{112,128},... | collective-permute-start | bytes 1544 | tf_op jit(solution)/shard_map/ppermute | solution.py:19
  81.8 1.0 copy-start.2
  84.4 26.2 %all-to-all-start.2 = ((bf16[32,2,2,2048]{3,2,1,0:T(2,128)(2,1)}), bf16[32,2,2,2048]{3,2,1,0:T(2,128)(2,1)}, u32[]{:S(2)}, u32[]{:S(2)}) async-start(bf16[32,2,2,2048]{3,2,1,0:T(2,128)(2,1)} %reshape.155), calls=%async_computation.2 | async-start | bytes 1048576 | tf_op jit(solution)/shard_map/all_to_all | solution.py:122
  116.1 113.2 %all-to-all-start.1 = ((bf16[32,16,1,2,2048]{4,3,0,2,1:T(2,128)(2,1)}), bf16[32,16,1,2,2048]{4,3,0,2,1:T(2,128)(2,1)}, u32[]{:S(2)}, u32[]{:S(2)}) async-start(bf16[32,16,1,2,2048]{4,3,0,2,1:T(2,128)(2,1)} %bitcast.126), calls=%async_computation.1 | async-start | bytes 8388608 | tf_op jit(solution)/shard_map/all_to_all | solution.py:130
  234.7 4.7 copy-start.5
  234.7 59.7 %all-to-all-start.3 = ((bf16[32,16,1,2,2048]{4,3,0,2,1:T(2,128)(2,1)}), bf16[32,16,1,2,2048]{4,3,0,2,1:T(2,128)(2,1)}, u32[]{:S(2)}, u32[]{:S(2)}) async-start(bf16[32,16,1,2,2048]{4,3,0,2,1:T(2,128)(2,1)} %bitcast.127), calls=%async_computation.3 | async-start | bytes 8388608 | tf_op jit(solution)/shard_map/all_to_all | solution.py:127
  245.1 55.1 %copy-start.6 = (bf16[2048,176]{0,1:T(8,128)(2,1)S(1)}, bf16[2048,176]{0,1:T(8,128)(2,1)}, u32[]{:S(2)}) copy-start(bf16[2048,176]{0,1:T(8,128)(2,1)} %param.18) | copy-start | bytes 2162692
where the time goes:
time: 506 us; the launch traced here: 505 us
  waiting for transfers between devices  206 us (41%)
  blocking collectives  171 us (34%)
  starting transfers between devices  57.9 us (11%)
  matrix products  31.8 us (6%)
  local copies, waits for them, and re-layouts  27.4 us (5%)
  other arithmetic  11.2 us (2%)
    all_to_all x1, blocking collectives, shards(): lax.all_to_all(summed, 'ctx', split_axis=0, concat_axis=0, tiled=True)  106 us
    all_to_all x1, waiting for transfers between devices, shards(): lax.all_to_all(spread_copies(owner_grads), 'ep', split_axis=1, concat_axi...  97 us
    all_to_all x1, blocking collectives, shards(): lax.all_to_all(partials, 'ep', split_axis=1, concat_axis=1, tiled=True)  64.9 us
    all_to_all x1, waiting for transfers between devices, shards(): lax.all_to_all(spread_copies(owner_normed), 'ep', split_axis=1, concat_ax...  49.3 us
    ppermute x4, waiting for transfers between devices, shifted(): lax.ppermute(value, axis, [(source, source + steps) for source in range(l...  46 us
    all_to_all x1, starting transfers between devices, shards(): lax.all_to_all(spread_copies(owner_grads), 'ep', split_axis=1, concat_axi...  14.7 us
    ppermute x4, starting transfers between devices, shifted(): lax.ppermute(value, axis, [(source, source + steps) for source in range(l...  13.8 us
    all_to_all x1, waiting for transfers between devices, shards(): lax.all_to_all(normed_slots, 'ctx', split_axis=0, concat_axis=0, tiled=True)  13.2 us
  transfers between devices with their start and end apart: 8, of which 5 were waited for; matrix products, arithmetic and copies ran while one was open for 3% of the time, Pallas kernels for 0%

commit v1 on v0

v1 whole, which is shorter than its diff:
```python
import functools
import math

import jax
import jax.numpy as jnp
from jax import lax
from jax.experimental import pallas as pl
from jax.experimental.pallas import tpu as pltpu
from jax.sharding import PartitionSpec as P

HEADS = 16
HEAD = 128
CAP = 2
ZL = 4
ZH = 2
XS = 4
CORES = 2
SLICES = XS * CORES
GROUP_HEADS = 2
LEAD = 3
HALVES = 2

F32 = jnp.float32
BF16 = jnp.bfloat16
MESH = pl.DeviceIdType.MESH


def nn(a, b):
    return lax.dot_general(a, b, (((1,), (0,)), ((), ())), preferred_element_type=F32)


def nt(a, b):
    return lax.dot_general(a, b, (((1,), (1,)), ((), ())), preferred_element_type=F32)


def scratch_of(tokens, width, slice_cols, ys):
    zs = ZL * ZH
    slots = ys * zs * CAP
    cols = GROUP_HEADS * HEAD
    groups = width // cols
    hidden_units = SLICES * slice_cols
    half = hidden_units // HALVES
    dma = pltpu.SemaphoreType.DMA
    chunked = pltpu.VMEM((groups, slots, cols), BF16)
    flat = pltpu.VMEM((slots, width), BF16)
    weights = pltpu.VMEM((hidden_units, width), BF16)
    return dict(
        q=pltpu.VMEM((groups, tokens, cols), BF16),
        kv=pltpu.VMEM((3, 2, groups, tokens, cols), BF16),
        tags=pltpu.VMEM((2, 1, tokens), jnp.int32),
        go=pltpu.VMEM((tokens, width), BF16),
        bias=pltpu.VMEM((3, tokens, tokens), F32),
        pick=pltpu.VMEM((slots, tokens), BF16),
        place=pltpu.VMEM((tokens, slots), BF16),
        perm_f=pltpu.VMEM((slots, slots), BF16),
        perm_r=pltpu.VMEM((slots, slots), BF16),
        g_send=flat, g_z=flat, g_mid=flat, g_y=flat,
        hid=pltpu.VMEM((groups, tokens, cols), BF16),
        h_send=chunked, h_z=chunked, h_mid=chunked, h_y=chunked,
        wg=weights, wu=weights, wd=weights,
        normed=flat,
        d_gate=pltpu.VMEM((HALVES, slots, half), BF16),
        d_up=pltpu.VMEM((HALVES, slots, half), BF16),
        r_send=chunked, r_y=chunked, r_mid=chunked, r_z=chunked,
        gained=pltpu.VMEM((groups, tokens, cols), F32),
        out_v=pltpu.VMEM((groups, tokens, cols), BF16),
        load_q=dma, load_kv=dma, load_go=dma, load_w=dma((3,)), store=dma,
        kv_s=dma((2, 2, groups)), kv_r=dma((2, 2, groups)),
        tag_s=dma((2,)), tag_r=dma((2,)),
        gz_s=dma, gz_r=dma, gy_s=dma, gy_r=dma,
        hz_s=dma((groups,)), hz_r=dma((groups,)), hy_s=dma((groups,)), hy_r=dma((groups,)),
        ry_s=dma((groups,)), ry_r=dma((groups,)), rz_s=dma((groups,)), rz_r=dma((groups,)),
        w_s=dma((3, 8)), w_r=dma((3, 8)),
    )


def kernel(
    names, doc_ref, route_ref, rw_ref, gain_ref,
    q_hbm, k_hbm, v_hbm, go_hbm, wg_hbm, wu_hbm, wd_hbm, out_hbm, *scratch,
):
    s = dict(zip(names, scratch))
    groups, tokens, cols = s["q"].shape
    slots = s["pick"].shape[0]
    width = groups * cols
    slice_cols = wd_hbm.shape[0]
    half = s["d_gate"].shape[2]
    ctx, ep = lax.axis_index("ctx"), lax.axis_index("ep")
    ctxs = lax.axis_size("ctx")
    ys, zs = ctxs // ZL, ZL * ZH
    y, z_lo = ctx // ZL, ctx % ZL
    z_hi, x, core = ep // (XS * CORES), (ep // CORES) % XS, ep % CORES
    z = z_hi * ZL + z_lo
    z_rows, y_rows = ys * CAP, zs * CAP

    def z_peer(t):
        return {"ctx": y * ZL + t % ZL, "ep": (t // ZL) * (XS * CORES) + x * CORES + core}

    def y_peer(t):
        return {"ctx": t * ZL + z_lo, "ep": ep}

    def x_peer(t, c):
        return {"ctx": ctx, "ep": z_hi * (XS * CORES) + (t % XS) * CORES + c}

    after = {"ctx": (ctx + 1) % ctxs, "ep": ep}
    before = {"ctx": (ctx + ctxs - 1) % ctxs, "ep": ep}
    right, left = x_peer(x + 1, core), x_peer(x + XS - 1, core)
    twin = x_peer(x, 1 - core)

    def order(count):
        steps = []
        for i in range(1, count // 2 + 1):
            steps.append(i)
            if count - i != i:
                steps.append(count - i)
        return steps

    barrier = pltpu.get_barrier_semaphore()
    peers = [after, before, right, left, twin]
    peers += [z_peer((z + i) % zs) for i in order(zs)]
    peers += [y_peer((y + i) % ys) for i in order(ys)]
    for peer in peers:
        pl.semaphore_signal(barrier, inc=1, device_id=peer, device_id_type=MESH)

    def local(src, dst, sem):
        pltpu.make_async_copy(src, dst, sem).start()

    def wait(ref, sem):
        pltpu.make_async_copy(ref, ref, sem).wait()

    def send(src, dst, s_sem, r_sem, peer):
        pltpu.make_async_remote_copy(
            src_ref=src, dst_ref=dst, send_sem=s_sem, recv_sem=r_sem,
            device_id=peer, device_id_type=MESH,
        ).start()

    def exchange(src, dst, rows, count, mine, peer, s_sem, r_sem):
        own = pl.ds(pl.multiple_of(mine * rows, rows), rows)
        for i in order(count):
            t = (mine + i) % count
            there = pl.ds(pl.multiple_of(t * rows, rows), rows)
            send(src.at[there], dst.at[own], s_sem, r_sem, peer(t))
        local(src.at[own], dst.at[own], r_sem)

    def sent(src, rows, count, s_sem):
        wait(src.at[pl.ds(0, rows * (count - 1))], s_sem)

    def col(g):
        return pl.ds(pl.multiple_of(g * cols, cols), cols)

    local(go_hbm.at[0], s["go"], s["load_go"])
    own_rows = pl.ds(0, slice_cols)
    for a, (ref, name) in enumerate(((wg_hbm, "wg"), (wu_hbm, "wu"), (wd_hbm, "wd"))):
        local(ref, s[name].at[own_rows], s["load_w"].at[a])

    @pl.loop(0, groups)
    def _(g):
        local(q_hbm.at[0, :, col(g)], s["q"].at[g], s["load_q"])
        local(k_hbm.at[0, :, col(g)], s["kv"].at[0, 0, g], s["load_kv"])
        local(v_hbm.at[0, :, col(g)], s["kv"].at[0, 1, g], s["load_kv"])

    def grid(shape, axis):
        return lax.broadcasted_iota(jnp.int32, shape, axis)

    def across(row):
        return jnp.transpose(jnp.broadcast_to(row.astype(F32), (tokens, tokens)))

    def onehot(mask):
        return jnp.where(mask, 1.0, 0.0).astype(BF16)

    square = (tokens, tokens)
    route_row = route_ref[...].astype(F32)
    same = (jnp.broadcast_to(route_row, square) == across(route_row)) & (
        grid(square, 0) < grid(square, 1)
    )
    rank = jnp.sum(jnp.where(same, 1.0, 0.0), axis=0, keepdims=True).astype(jnp.int32)
    expert = route_ref[...]
    bits_zh, bits_zl = ZH.bit_length() - 1, ZL.bit_length() - 1
    dest_y = lax.shift_right_logical(expert, bits_zh + bits_zl)
    dest_z = (expert & (ZH - 1)) * ZL + (lax.shift_right_logical(expert, bits_zh) & (ZL - 1))
    target = jnp.where(rank < CAP, dest_z * z_rows + dest_y * CAP + rank, -1)
    s["pick"][...] = onehot(jnp.broadcast_to(target, (slots, tokens)) == grid((slots, tokens), 0))
    s["place"][...] = onehot(across(target) == grid((tokens, slots), 1).astype(F32))

    def regroup(index, outer, inner):
        bits_o, bits_i = outer.bit_length() - 1, inner.bit_length() - 1
        o = lax.shift_right_logical(index, bits_i + 1)
        i = lax.shift_right_logical(index, 1) & (inner - 1)
        return i * (outer * CAP) + o * CAP + (index & (CAP - 1))

    pairs = (slots, slots)
    s["perm_f"][...] = onehot(regroup(grid(pairs, 0), ys, zs) == grid(pairs, 1))
    s["perm_r"][...] = onehot(regroup(grid(pairs, 0), zs, ys) == grid(pairs, 1))

    pl.semaphore_wait(barrier, len(peers))

    def send_own(g):
        for part, ref in ((0, k_hbm), (1, v_hbm)):
            send(
                ref.at[0, :, col(g)], s["kv"].at[1, part, g],
                s["kv_s"].at[0, part, g], s["kv_r"].at[0, part, g], after,
            )

    for g in range(min(LEAD, groups)):
        send_own(g)
    send(doc_ref, s["tags"].at[0], s["tag_s"].at[0], s["tag_r"].at[0], after)

    gathered = (s["wg"], s["wu"], s["wd"])

    def part_of(slot):
        return pl.ds(slot * slice_cols, slice_cols)

    def weights_out(a, src):
        ref = gathered[a]
        send(src, ref.at[part_of(2)], s["w_s"].at[a, 0], s["w_r"].at[a, 0], right)
        send(src, ref.at[part_of(4)], s["w_s"].at[a, 1], s["w_r"].at[a, 1], left)
        send(src, ref.at[part_of(1)], s["w_s"].at[a, 2], s["w_r"].at[a, 2], twin)

    first_cols, last_cols = pl.ds(0, width // 2), pl.ds(width // 2, width // 2)

    def weights_relay(a):
        ref = gathered[a]
        wait(ref.at[part_of(2)], s["w_r"].at[a, 0])
        send(
            ref.at[part_of(2), first_cols], ref.at[part_of(6), first_cols],
            s["w_s"].at[a, 3], s["w_r"].at[a, 3], right,
        )
        send(ref.at[part_of(2)], ref.at[part_of(3)], s["w_s"].at[a, 5], s["w_r"].at[a, 5], twin)
        wait(ref.at[part_of(4)], s["w_r"].at[a, 1])
        send(
            ref.at[part_of(4), last_cols], ref.at[part_of(6), last_cols],
            s["w_s"].at[a, 4], s["w_r"].at[a, 4], left,
        )
        send(ref.at[part_of(4)], ref.at[part_of(5)], s["w_s"].at[a, 6], s["w_r"].at[a, 6], twin)

    def weights_last(a):
        ref = gathered[a]
        wait(ref.at[part_of(6), first_cols], s["w_r"].at[a, 3])
        wait(ref.at[part_of(6), last_cols], s["w_r"].at[a, 4])
        send(ref.at[part_of(6)], ref.at[part_of(7)], s["w_s"].at[a, 7], s["w_r"].at[a, 7], twin)

    def weights_in(a):
        ref = gathered[a]
        for slot, r in ((1, 2), (3, 5), (5, 6), (7, 7)):
            wait(ref.at[part_of(slot)], s["w_r"].at[a, r])
        for k in (0, 1, 2, 5, 6, 7):
            wait(ref.at[part_of(0)], s["w_s"].at[a, k])
        wait(ref.at[part_of(0), first_cols], s["w_s"].at[a, 3])
        wait(ref.at[part_of(0), last_cols], s["w_s"].at[a, 4])

    for a, ref in ((2, wd_hbm), (0, wg_hbm), (1, wu_hbm)):
        weights_out(a, ref)

    wait(s["go"], s["load_go"])
    weight_col = across(rw_ref[...])[:, :1]
    for g in range(groups):
        at = pl.ds(g * cols, cols)
        rows = (weight_col * s["go"][:, at].astype(F32)).astype(BF16)
        s["g_send"][:, at] = nn(s["pick"][...], rows).astype(BF16)
    exchange(s["g_send"], s["g_z"], z_rows, zs, z, z_peer, s["gz_s"], s["gz_r"])

    wait(s["q"], s["load_q"])
    wait(s["kv"].at[0], s["load_kv"])
    scale = 1.0 / math.sqrt(HEAD)

    def attend(g):
        for h in range(GROUP_HEADS):
            at = slice(h * HEAD, (h + 1) * HEAD)
            query = s["q"][g][:, at]
            scores = [
                nt(query, s["kv"][d, 0, g][:, at]) * scale + s["bias"][d] for d in range(3)
            ]
            top = jnp.max(
                jnp.maximum(jnp.maximum(scores[0], scores[1]), scores[2]), axis=-1, keepdims=True
            )
            raised = [jnp.exp(one - top) for one in scores]
            total = jnp.sum(raised[0] + raised[1] + raised[2], axis=-1, keepdims=True)
            share = 1.0 / total
            mixed = None
            for d in range(3):
                term = nn((raised[d] * share).astype(BF16), s["kv"][d, 1, g][:, at])
                mixed = term if mixed is None else mixed + term
            s["hid"][g, :, at] = mixed.astype(BF16)
        s["h_send"][g] = nn(s["pick"][...], s["hid"][g]).astype(BF16)

    @pl.loop(0, groups + 3)
    def _(step):
        @pl.when(step < groups)
        def _():
            for part in range(2):
                here = s["kv"].at[1, part, step]
                wait(here, s["kv_r"].at[0, part, step])
                send(
                    here, s["kv"].at[2, part, step],
                    s["kv_s"].at[1, part, step], s["kv_r"].at[1, part, step], after,
                )

        @pl.when(step + LEAD < groups)
        def _():
            send_own(step + LEAD)

        @pl.when(step == 0)
        def _():
            wait(s["tags"].at[0], s["tag_r"].at[0])
            send(s["tags"].at[0], s["tags"].at[1], s["tag_s"].at[1], s["tag_r"].at[1], after)

        @pl.when(step == 1)
        def _():
            wait(s["tags"].at[1], s["tag_r"].at[1])
            doc_col = across(doc_ref[...])
            for d in range(3):
                row = doc_ref[...] if d == 0 else s["tags"][d - 1]
                seen = row.astype(F32) - jnp.where(ctx >= d, 0.0, 1e6)
                open_ = doc_col == jnp.broadcast_to(seen, square)
                if d == 0:
                    open_ = open_ & (grid(square, 1) <= grid(square, 0))
                s["bias"][d] = jnp.where(open_, 0.0, -1e30)

        @pl.when((step >= 1) & (step <= groups))
        def _():
            g = step - 1
            for part in range(2):
                wait(s["kv"].at[2, part, g], s["kv_r"].at[1, part, g])
            attend(g)
            exchange(
                s["h_send"].at[g], s["h_z"].at[g], z_rows, zs, z, z_peer,
                s["hz_s"].at[g], s["hz_r"].at[g],
            )

        @pl.when(step >= 3)
        def _():
            g = step - 3
            wait(s["h_z"].at[g], s["hz_r"].at[g])
            s["h_mid"][g] = nn(s["perm_f"][...], s["h_z"][g]).astype(BF16)
            exchange(
                s["h_mid"].at[g], s["h_y"].at[g], y_rows, ys, y, y_peer,
                s["hy_s"].at[g], s["hy_r"].at[g],
            )

        @pl.when(step == 3)
        def _():
            wait(s["g_z"], s["gz_r"])
            for g in range(groups):
                at = pl.ds(g * cols, cols)
                s["g_mid"][:, at] = nn(s["perm_f"][...], s["g_z"][:, at]).astype(BF16)
            exchange(s["g_mid"], s["g_y"], y_rows, ys, y, y_peer, s["gy_s"], s["gy_r"])

        for a, when in ((2, 2), (0, 5), (1, 8)):

            @pl.when(step == min(when, groups + 2))
            def _():
                weights_relay(a)

    squares = None
    for g in range(groups):
        one = s["hid"][g].astype(F32)
        one = jnp.sum(one * one, axis=-1, keepdims=True)
        squares = one if squares is None else squares + one
    inv_rms = lax.rsqrt(squares * (1.0 / width) + 1e-06)

    for a in (2, 0, 1):
        weights_last(a)

    squares = None
    for g in range(groups):
        wait(s["h_y"].at[g], s["hy_r"].at[g])
        one = s["h_y"][g].astype(F32)
        one = jnp.sum(one * one, axis=-1, keepdims=True)
        squares = one if squares is None else squares + one
    inv_there = lax.rsqrt(squares * (1.0 / width) + 1e-06)
    for g in range(groups):
        at = pl.ds(g * cols, cols)
        s["normed"][:, at] = (s["h_y"][g].astype(F32) * inv_there * gain_ref[:, at]).astype(BF16)
    wait(s["g_y"], s["gy_r"])
    for a in (2, 0, 1):
        wait(gathered[a].at[own_rows], s["load_w"].at[a])
        weights_in(a)

    @pl.loop(0, HALVES)
    def _(part):
        rows = pl.ds(pl.multiple_of(part * half, half), half)
        gate_pre = nt(s["normed"][...], s["wg"][rows, :])
        up_pre = nt(s["normed"][...], s["wu"][rows, :])
        grad_act = nt(s["g_y"][...], s["wd"][rows, :])
        sg = 1.0 / (1.0 + jnp.exp(-gate_pre))
        s["d_gate"][part] = (
            grad_act * up_pre * (sg * (1.0 + gate_pre * (1.0 - sg)))
        ).astype(BF16)
        s["d_up"][part] = (grad_act * (gate_pre * sg)).astype(BF16)

    @pl.loop(0, groups + 2)
    def _(step):
        @pl.when(step < groups)
        def _():
            total = None
            for part in range(HALVES):
                rows = pl.ds(part * half, half)
                for rows_in, ref in ((s["d_gate"], s["wg"]), (s["d_up"], s["wu"])):
                    term = nn(rows_in[part], ref[rows, col(step)])
                    total = term if total is None else total + term
            s["r_send"][step] = total.astype(BF16)
            exchange(
                s["r_send"].at[step], s["r_y"].at[step], y_rows, ys, y, y_peer,
                s["ry_s"].at[step], s["ry_r"].at[step],
            )

        @pl.when(step >= 2)
        def _():
            g = step - 2
            wait(s["r_y"].at[g], s["ry_r"].at[g])
            s["r_mid"][g] = nn(s["perm_r"][...], s["r_y"][g]).astype(BF16)
            exchange(
                s["r_mid"].at[g], s["r_z"].at[g], z_rows, zs, z, z_peer,
                s["rz_s"].at[g], s["rz_r"].at[g],
            )

    along = None
    for g in range(groups):
        wait(s["r_z"].at[g], s["rz_r"].at[g])
        gained = nn(s["place"][...], s["r_z"][g]) * gain_ref[:, pl.ds(g * cols, cols)]
        s["gained"][g] = gained
        one = jnp.sum(s["hid"][g].astype(F32) * gained, axis=-1, keepdims=True)
        along = one if along is None else along + one
    slope = inv_rms * inv_rms * inv_rms * (along * (1.0 / width))
    for g in range(groups):
        at = pl.ds(g * cols, cols)
        s["out_v"][g] = (
            s["go"][:, at].astype(F32)
            + inv_rms * s["gained"][g]
            - s["hid"][g].astype(F32) * slope
        ).astype(BF16)
        local(s["out_v"].at[g], out_hbm.at[0, :, at], s["store"])

    @pl.loop(0, groups)
    def _(g):
        for hop in range(2):
            for part in range(2):
                wait(s["kv"].at[hop, part, g], s["kv_s"].at[hop, part, g])
        sent(s["h_send"].at[g], z_rows, zs, s["hz_s"].at[g])
        sent(s["h_mid"].at[g], y_rows, ys, s["hy_s"].at[g])
        sent(s["r_send"].at[g], y_rows, ys, s["ry_s"].at[g])
        sent(s["r_mid"].at[g], z_rows, zs, s["rz_s"].at[g])

    for hop in range(2):
        wait(s["tags"].at[hop], s["tag_s"].at[hop])
    sent(s["g_send"], z_rows, zs, s["gz_s"])
    sent(s["g_mid"], y_rows, ys, s["gy_s"])
    wait(s["out_v"], s["store"])


def shards(
    queries, keys, values, doc_ids, routes, route_weight, norm_gain, w_gate, w_up, w_down, grad_out
):
    tokens, width = queries.shape[1:]
    ys = lax.axis_size("ctx") // ZL
    scratch = scratch_of(tokens, width, w_gate.shape[1], ys)
    small = pl.BlockSpec(memory_space=pltpu.VMEM)
    large = pl.BlockSpec(memory_space=pl.ANY)
    return pl.pallas_call(
        functools.partial(kernel, tuple(scratch)),
        out_shape=jax.ShapeDtypeStruct(grad_out.shape, BF16),
        in_specs=[small] * 4 + [large] * 7,
        out_specs=large,
        scratch_shapes=list(scratch.values()),
        compiler_params=pltpu.CompilerParams(
            collective_id=0, has_side_effects=True, vmem_limit_bytes=60 * 1024 * 1024
        ),
        name="layer",
    )(
        doc_ids,
        routes.reshape(1, tokens),
        route_weight.reshape(1, tokens),
        norm_gain.reshape(1, width),
        queries, keys, values, grad_out, w_gate.T, w_up.T, w_down,
    )


def solution(mesh):
    rows = P("ep", "ctx", None)
    in_specs = (
        rows, rows, rows, P("ep", "ctx"), rows, rows, P(),
        P(None, ("ctx", "ep")), P(None, ("ctx", "ep")), P(("ctx", "ep"), None), rows,
    )
    return jax.shard_map(shards, mesh=mesh, in_specs=in_specs, out_specs=rows, check_vma=False)
```

time: 506 us -> 146 us (0.29)
  waiting for transfers between devices: 206 us -> 0 us
  blocking collectives: 171 us -> 0 us
  Pallas kernels: 0 us -> 144 us
  starting transfers between devices: 57.9 us -> 0 us
  matrix products: 31.8 us -> 0 us
  local copies, waits for them, and re-layouts: 27.4 us -> 1.88 us
  other arithmetic: 11.2 us -> 0 us
    all_to_all x2 -> x0, blocking collectives: 171 us -> none  [the longest x1 106 us: shards(): lax.all_to_all(summed, 'ctx', split_axis=0, concat_axis=0, tiled=True)]
    all_to_all x4 -> x0, waiting for transfers between devices: 160 us -> none  [the longest x1 97 us: shards(): lax.all_to_all(spread_copies(owner_grads), 'ep', split_axis=1, concat_axi...]
    pallas_call x0 -> x1, Pallas kernels: none -> 144 us  [shards(): pl.pallas_call(functools.partial(kernel, tuple(scratch)), out_shape=jax.S...]
    ppermute x4 -> x0, waiting for transfers between devices: 46 us -> none  [shifted(): lax.ppermute(value, axis, [(source, source + steps) for source in range(l...]
    all_to_all x4 -> x0, starting transfers between devices: 44 us -> none  [the longest x1 14.7 us: shards(): lax.all_to_all(spread_copies(owner_grads), 'ep', split_axis=1, concat_axi...]
    dot_general x9 -> x0, matrix products: 31.8 us -> none  [the longest x1 10.7 us: expert_piece(): jnp.einsum('aeqkw,dqw->aeqkd', grad_gate, gate_piece, preferred_element_t...]
    ppermute x4 -> x0, starting transfers between devices: 13.8 us -> none  [shifted(): lax.ppermute(value, axis, [(source, source + steps) for source in range(l...]
    broadcast_in_dim x2 -> x0, local copies, waits for them, and re-layouts: 11 us -> none  [spread_copies(): jnp.broadcast_to(slots[:, :, None], (slots.shape[0], groups, per_expert,...]
  transfers between devices with their start and end apart: 8 -> 0, of which waited for: 5 -> 0; matrix products, arithmetic and copies ran while one was open for 3% -> 0% of each run, Pallas kernels for 0% -> 0%
where the time goes in v1:
time: 146 us
  Pallas kernels  144 us (99%)
  local copies, waits for them, and re-layouts  1.88 us (1%)
    pallas_call x1, Pallas kernels, shards(): pl.pallas_call(functools.partial(kernel, tuple(scratch)), out_shape=jax.S...  144 us

profile of v1, /device:TPU:8, one launch (start us, length us, event | category | flops | bytes accessed | tf_op | source)
XLA Modules:
  0.0 146.2 jit_solution(1771432507685669091)
XLA Ops:
  0.0 144.3 %layer.1 = bf16[1,128,2048]{2,1,0:T(8,128)(2,1)} custom-call(s32[1,128]{1,0:T(1,128)} %doc_ref.1, s32[1,128]{1,0:T(1,128)} %bitcast.8, f32[1,128]{1,0:T(1,128)} %bitcast.9, f32[1,2048]{1,0:T(1,128)} %bitcast.7, bf16[1,128,2048]{2,1,0:T(8,128)(2,1)} %q_hbm.1, bf16[1,128,2048]{2,1,0:T(8,128)(2,1)} %k_hbm.1, bf16[1,128,2048]{2,1,0:T(8,128)(2,1)} %v_hbm.1, ...), custom_call_target="tpu_custom_call" | custom-call | tf_op jit(solution)/shard_map/layer/pallas_call | solution.py:458
  144.3 1.9 %copy.13 = bf16[1,128,2048]{2,1,0:T(8,128)(2,1)} copy(bf16[1,128,2048]{2,1,0:T(8,128)(2,1)} %layer.1) | data formatting | bytes 1048576

commit v2 on v1

--- a/solution.py
+++ b/solution.py
@@ -51,25 +51,26 @@
         go=pltpu.VMEM((tokens, width), BF16),
         bias=pltpu.VMEM((3, tokens, tokens), F32),
         pick=pltpu.VMEM((slots, tokens), BF16),
-        place=pltpu.VMEM((tokens, slots), BF16),
+        place=pltpu.VMEM((2, tokens, slots), BF16),
         perm_f=pltpu.VMEM((slots, slots), BF16),
         perm_r=pltpu.VMEM((slots, slots), BF16),
-        g_send=flat, g_z=flat, g_mid=flat, g_y=flat,
+        g_send=chunked, g_z=chunked, g_mid=chunked, g_y=flat,
         hid=pltpu.VMEM((groups, tokens, cols), BF16),
         h_send=chunked, h_z=chunked, h_mid=chunked, h_y=chunked,
         wg=weights, wu=weights, wd=weights,
         normed=flat,
+        d_act=pltpu.VMEM((HALVES, slots, half), F32),
         d_gate=pltpu.VMEM((HALVES, slots, half), BF16),
         d_up=pltpu.VMEM((HALVES, slots, half), BF16),
-        r_send=chunked, r_y=chunked, r_mid=chunked, r_z=chunked,
+        r_send=chunked, r_one=chunked, r_mid=chunked, r_two=chunked,
         gained=pltpu.VMEM((groups, tokens, cols), F32),
         out_v=pltpu.VMEM((groups, tokens, cols), BF16),
         load_q=dma, load_kv=dma, load_go=dma, load_w=dma((3,)), store=dma,
         kv_s=dma((2, 2, groups)), kv_r=dma((2, 2, groups)),
         tag_s=dma((2,)), tag_r=dma((2,)),
-        gz_s=dma, gz_r=dma, gy_s=dma, gy_r=dma,
+        gz_s=dma((groups,)), gz_r=dma((groups,)), gy_s=dma((groups,)), gy_r=dma((groups,)),
         hz_s=dma((groups,)), hz_r=dma((groups,)), hy_s=dma((groups,)), hy_r=dma((groups,)),
-        ry_s=dma((groups,)), ry_r=dma((groups,)), rz_s=dma((groups,)), rz_r=dma((groups,)),
+        r1_s=dma((groups,)), r1_r=dma((groups,)), r2_s=dma((groups,)), r2_r=dma((groups,)),
         w_s=dma((3, 8)), w_r=dma((3, 8)),
     )
 
@@ -179,7 +180,9 @@
     dest_z = (expert & (ZH - 1)) * ZL + (lax.shift_right_logical(expert, bits_zh) & (ZL - 1))
     target = jnp.where(rank < CAP, dest_z * z_rows + dest_y * CAP + rank, -1)
     s["pick"][...] = onehot(jnp.broadcast_to(target, (slots, tokens)) == grid((slots, tokens), 0))
-    s["place"][...] = onehot(across(target) == grid((tokens, slots), 1).astype(F32))
+    target_y = jnp.where(rank < CAP, dest_y * y_rows + dest_z * CAP + rank, -1)
+    for i, at in enumerate((target, target_y)):
+        s["place"][i] = onehot(across(at) == grid((tokens, slots), 1).astype(F32))
 
     def regroup(index, outer, inner):
         bits_o, bits_i = outer.bit_length() - 1, inner.bit_length() - 1
@@ -255,8 +258,7 @@
     for g in range(groups):
         at = pl.ds(g * cols, cols)
         rows = (weight_col * s["go"][:, at].astype(F32)).astype(BF16)
-        s["g_send"][:, at] = nn(s["pick"][...], rows).astype(BF16)
-    exchange(s["g_send"], s["g_z"], z_rows, zs, z, z_peer, s["gz_s"], s["gz_r"])
+        s["g_send"][g] = nn(s["pick"][...], rows).astype(BF16)
 
     wait(s["q"], s["load_q"])
     wait(s["kv"].at[0], s["load_kv"])
@@ -282,7 +284,7 @@
             s["hid"][g, :, at] = mixed.astype(BF16)
         s["h_send"][g] = nn(s["pick"][...], s["hid"][g]).astype(BF16)
 
-    @pl.loop(0, groups + 3)
+    @pl.loop(0, groups + 4)
     def _(step):
         @pl.when(step < groups)
         def _():
@@ -315,9 +317,9 @@
                     open_ = open_ & (grid(square, 1) <= grid(square, 0))
                 s["bias"][d] = jnp.where(open_, 0.0, -1e30)
 
-        @pl.when((step >= 1) & (step <= groups))
+        @pl.when((step >= 2) & (step < groups + 2))
         def _():
-            g = step - 1
+            g = step - 2
             for part in range(2):
                 wait(s["kv"].at[2, part, g], s["kv_r"].at[1, part, g])
             attend(g)
@@ -325,10 +327,20 @@
                 s["h_send"].at[g], s["h_z"].at[g], z_rows, zs, z, z_peer,
                 s["hz_s"].at[g], s["hz_r"].at[g],
             )
-
-        @pl.when(step >= 3)
+            exchange(
+                s["g_send"].at[g], s["g_z"].at[g], z_rows, zs, z, z_peer,
+                s["gz_s"].at[g], s["gz_r"].at[g],
+            )
+
+        @pl.when(step >= 4)
         def _():
-            g = step - 3
+            g = step - 4
+            wait(s["g_z"].at[g], s["gz_r"].at[g])
+            s["g_mid"][g] = nn(s["perm_f"][...], s["g_z"][g]).astype(BF16)
+            exchange(
+                s["g_mid"].at[g], s["g_y"].at[:, col(g)], y_rows, ys, y, y_peer,
+                s["gy_s"].at[g], s["gy_r"].at[g],
+            )
             wait(s["h_z"].at[g], s["hz_r"].at[g])
             s["h_mid"][g] = nn(s["perm_f"][...], s["h_z"][g]).astype(BF16)
             exchange(
@@ -336,19 +348,17 @@
                 s["hy_s"].at[g], s["hy_r"].at[g],
             )
 
-        @pl.when(step == 3)
-        def _():
-            wait(s["g_z"], s["gz_r"])
-            for g in range(groups):
-                at = pl.ds(g * cols, cols)
-                s["g_mid"][:, at] = nn(s["perm_f"][...], s["g_z"][:, at]).astype(BF16)
-            exchange(s["g_mid"], s["g_y"], y_rows, ys, y, y_peer, s["gy_s"], s["gy_r"])
-
-        for a, when in ((2, 2), (0, 5), (1, 8)):
-
-            @pl.when(step == min(when, groups + 2))
+        for a, when in ((2, 2), (0, 4), (1, 6)):
+
+            @pl.when(step == min(when, groups))
             def _():
                 weights_relay(a)
+
+        for a, when in ((2, 2), (0, 1)):
+
+            @pl.when(step == groups + 3 - when)
+            def _():
+                weights_last(a)
 
     squares = None
     for g in range(groups):
@@ -357,8 +367,22 @@
         squares = one if squares is None else squares + one
     inv_rms = lax.rsqrt(squares * (1.0 / width) + 1e-06)
 
-    for a in (2, 0, 1):
-        weights_last(a)
+    weights_last(1)
+
+    def all_here(a):
+        wait(gathered[a].at[own_rows], s["load_w"].at[a])
+        weights_in(a)
+
+    for g in range(groups):
+        wait(s["g_y"].at[:, pl.ds(g * cols, cols)], s["gy_r"].at[g])
+    all_here(2)
+
+    def units(part):
+        return pl.ds(pl.multiple_of(part * half, half), half)
+
+    @pl.loop(0, HALVES)
+    def _(part):
+        s["d_act"][part] = nt(s["g_y"][...], s["wd"][units(part), :])
 
     squares = None
     for g in range(groups):
@@ -370,53 +394,59 @@
     for g in range(groups):
         at = pl.ds(g * cols, cols)
         s["normed"][:, at] = (s["h_y"][g].astype(F32) * inv_there * gain_ref[:, at]).astype(BF16)
-    wait(s["g_y"], s["gy_r"])
-    for a in (2, 0, 1):
-        wait(gathered[a].at[own_rows], s["load_w"].at[a])
-        weights_in(a)
+    all_here(0)
+    all_here(1)
 
     @pl.loop(0, HALVES)
     def _(part):
-        rows = pl.ds(pl.multiple_of(part * half, half), half)
-        gate_pre = nt(s["normed"][...], s["wg"][rows, :])
-        up_pre = nt(s["normed"][...], s["wu"][rows, :])
-        grad_act = nt(s["g_y"][...], s["wd"][rows, :])
+        gate_pre = nt(s["normed"][...], s["wg"][units(part), :])
+        up_pre = nt(s["normed"][...], s["wu"][units(part), :])
+        grad_act = s["d_act"][part]
         sg = 1.0 / (1.0 + jnp.exp(-gate_pre))
         s["d_gate"][part] = (
             grad_act * up_pre * (sg * (1.0 + gate_pre * (1.0 - sg)))
         ).astype(BF16)
         s["d_up"][part] = (grad_act * (gate_pre * sg)).astype(BF16)
 
-    @pl.loop(0, groups + 2)
-    def _(step):
-        @pl.when(step < groups)
-        def _():
+    ways = (
+        (y_rows, ys, y, y_peer, z_rows, zs, z, z_peer, "perm_r"),
+        (z_rows, zs, z, z_peer, y_rows, ys, y, y_peer, "perm_f"),
+    )
+
+    @pl.loop(0, groups // 2)
+    def _(pair):
+        for way, (rows, count, mine, peer, *_) in enumerate(ways):
+            g = 2 * pair + way
             total = None
             for part in range(HALVES):
-                rows = pl.ds(part * half, half)
+                here = pl.ds(part * half, half)
                 for rows_in, ref in ((s["d_gate"], s["wg"]), (s["d_up"], s["wu"])):
-                    term = nn(rows_in[part], ref[rows, col(step)])
+                    term = nn(rows_in[part], ref[here, col(g)])
                     total = term if total is None else total + term
-            s["r_send"][step] = total.astype(BF16)
+            total = total.astype(BF16)
+            if way:
+                total = nn(s["perm_r"][...], total).astype(BF16)
+            s["r_send"][g] = total
             exchange(
-                s["r_send"].at[step], s["r_y"].at[step], y_rows, ys, y, y_peer,
-                s["ry_s"].at[step], s["ry_r"].at[step],
-            )
-
-        @pl.when(step >= 2)
-        def _():
-            g = step - 2
-            wait(s["r_y"].at[g], s["ry_r"].at[g])
-            s["r_mid"][g] = nn(s["perm_r"][...], s["r_y"][g]).astype(BF16)
+                s["r_send"].at[g], s["r_one"].at[g], rows, count, mine, peer,
+                s["r1_s"].at[g], s["r1_r"].at[g],
+            )
+
+    @pl.loop(0, groups // 2)
+    def _(pair):
+        for way, (*_, rows, count, mine, peer, perm) in enumerate(ways):
+            g = 2 * pair + way
+            wait(s["r_one"].at[g], s["r1_r"].at[g])
+            s["r_mid"][g] = nn(s[perm][...], s["r_one"][g]).astype(BF16)
             exchange(
-                s["r_mid"].at[g], s["r_z"].at[g], z_rows, zs, z, z_peer,
-                s["rz_s"].at[g], s["rz_r"].at[g],
+                s["r_mid"].at[g], s["r_two"].at[g], rows, count, mine, peer,
+                s["r2_s"].at[g], s["r2_r"].at[g],
             )
 
     along = None
     for g in range(groups):
-        wait(s["r_z"].at[g], s["rz_r"].at[g])
-        gained = nn(s["place"][...], s["r_z"][g]) * gain_ref[:, pl.ds(g * cols, cols)]
+        wait(s["r_two"].at[g], s["r2_r"].at[g])
+        gained = nn(s["place"][g % 2], s["r_two"][g]) * gain_ref[:, pl.ds(g * cols, cols)]
         s["gained"][g] = gained
         one = jnp.sum(s["hid"][g].astype(F32) * gained, axis=-1, keepdims=True)
         along = one if along is None else along + one
@@ -435,15 +465,20 @@
         for hop in range(2):
             for part in range(2):
                 wait(s["kv"].at[hop, part, g], s["kv_s"].at[hop, part, g])
+        sent(s["g_send"].at[g], z_rows, zs, s["gz_s"].at[g])
+        sent(s["g_mid"].at[g], y_rows, ys, s["gy_s"].at[g])
         sent(s["h_send"].at[g], z_rows, zs, s["hz_s"].at[g])
         sent(s["h_mid"].at[g], y_rows, ys, s["hy_s"].at[g])
-        sent(s["r_send"].at[g], y_rows, ys, s["ry_s"].at[g])
-        sent(s["r_mid"].at[g], z_rows, zs, s["rz_s"].at[g])
+
+    @pl.loop(0, groups // 2)
+    def _(pair):
+        for way, (rows, count, _, _, rows_2, count_2, *_) in enumerate(ways):
+            g = 2 * pair + way
+            sent(s["r_send"].at[g], rows, count, s["r1_s"].at[g])
+            sent(s["r_mid"].at[g], rows_2, count_2, s["r2_s"].at[g])
 
     for hop in range(2):
         wait(s["tags"].at[hop], s["tag_s"].at[hop])
-    sent(s["g_send"], z_rows, zs, s["gz_s"])
-    sent(s["g_mid"], y_rows, ys, s["gy_s"])
     wait(s["out_v"], s["store"])
 
 

time: 146 us -> 122 us (0.84)
  the two profiles are of different devices: /device:TPU:8 before, /device:TPU:2 now
where the time goes in v2:
time: 122 us
  Pallas kernels  120 us (98%)
  local copies, waits for them, and re-layouts  1.88 us (2%)
    pallas_call x1, Pallas kernels, shards(): pl.pallas_call(functools.partial(kernel, tuple(scratch)), out_shape=jax.S...  120 us

profile of v2, /device:TPU:2, one launch (start us, length us, event | category | flops | bytes accessed | tf_op | source)
XLA Modules:
  0.0 121.7 jit_solution(9095036878407585410)
XLA Ops:
  0.0 119.8 %layer.1 = bf16[1,128,2048]{2,1,0:T(8,128)(2,1)} custom-call(s32[1,128]{1,0:T(1,128)} %doc_ref.1, s32[1,128]{1,0:T(1,128)} %bitcast.8, f32[1,128]{1,0:T(1,128)} %bitcast.9, f32[1,2048]{1,0:T(1,128)} %bitcast.7, bf16[1,128,2048]{2,1,0:T(8,128)(2,1)} %q_hbm.1, bf16[1,128,2048]{2,1,0:T(8,128)(2,1)} %k_hbm.1, bf16[1,128,2048]{2,1,0:T(8,128)(2,1)} %v_hbm.1, ...), custom_call_target="tpu_custom_call" | custom-call | tf_op jit(solution)/shard_map/layer/pallas_call | solution.py:493
  119.9 1.9 %copy.13 = bf16[1,128,2048]{2,1,0:T(8,128)(2,1)} copy(bf16[1,128,2048]{2,1,0:T(8,128)(2,1)} %layer.1) | data formatting | bytes 1048576

commit v3 on v2

--- a/solution.py
+++ b/solution.py
@@ -113,7 +113,7 @@
             steps.append(i)
             if count - i != i:
                 steps.append(count - i)
-        return steps
+        return steps[::-1]
 
     barrier = pltpu.get_barrier_semaphore()
     peers = [after, before, right, left, twin]
@@ -284,6 +284,12 @@
             s["hid"][g, :, at] = mixed.astype(BF16)
         s["h_send"][g] = nn(s["pick"][...], s["hid"][g]).astype(BF16)
 
+    def send_g(g):
+        exchange(
+            s["g_send"].at[g], s["g_z"].at[g], z_rows, zs, z, z_peer,
+            s["gz_s"].at[g], s["gz_r"].at[g],
+        )
+
     @pl.loop(0, groups + 4)
     def _(step):
         @pl.when(step < groups)
@@ -320,16 +326,13 @@
         @pl.when((step >= 2) & (step < groups + 2))
         def _():
             g = step - 2
+            send_g(g)
             for part in range(2):
                 wait(s["kv"].at[2, part, g], s["kv_r"].at[1, part, g])
             attend(g)
             exchange(
                 s["h_send"].at[g], s["h_z"].at[g], z_rows, zs, z, z_peer,
                 s["hz_s"].at[g], s["hz_r"].at[g],
-            )
-            exchange(
-                s["g_send"].at[g], s["g_z"].at[g], z_rows, zs, z, z_peer,
-                s["gz_s"].at[g], s["gz_r"].at[g],
             )
 
         @pl.when(step >= 4)

time: 122 us -> 120 us (0.984)
  the two profiles are of different devices: /device:TPU:2 before, /device:TPU:4 now
where the time goes in v3:
time: 120 us
  Pallas kernels  118 us (98%)
  local copies, waits for them, and re-layouts  1.88 us (2%)
    pallas_call x1, Pallas kernels, shards(): pl.pallas_call(functools.partial(kernel, tuple(scratch)), out_shape=jax.S...  118 us

profile of v3, /device:TPU:4, one launch (start us, length us, event | category | flops | bytes accessed | tf_op | source)
XLA Modules:
  0.0 119.7 jit_solution(451472079271851759)
XLA Ops:
  0.0 117.8 %layer.1 = bf16[1,128,2048]{2,1,0:T(8,128)(2,1)} custom-call(s32[1,128]{1,0:T(1,128)} %doc_ref.1, s32[1,128]{1,0:T(1,128)} %bitcast.8, f32[1,128]{1,0:T(1,128)} %bitcast.9, f32[1,2048]{1,0:T(1,128)} %bitcast.7, bf16[1,128,2048]{2,1,0:T(8,128)(2,1)} %q_hbm.1, bf16[1,128,2048]{2,1,0:T(8,128)(2,1)} %k_hbm.1, bf16[1,128,2048]{2,1,0:T(8,128)(2,1)} %v_hbm.1, ...), custom_call_target="tpu_custom_call" | custom-call | tf_op jit(solution)/shard_map/layer/pallas_call | solution.py:496
  117.8 1.9 %copy.13 = bf16[1,128,2048]{2,1,0:T(8,128)(2,1)} copy(bf16[1,128,2048]{2,1,0:T(8,128)(2,1)} %layer.1) | data formatting | bytes 1048576

commit v4 on v2

--- a/solution.py
+++ b/solution.py
@@ -18,6 +18,8 @@
 SLICES = XS * CORES
 GROUP_HEADS = 2
 LEAD = 3
+G_LAG = 4
+G_START = 2
 HALVES = 2
 
 F32 = jnp.float32
@@ -50,11 +52,11 @@
         tags=pltpu.VMEM((2, 1, tokens), jnp.int32),
         go=pltpu.VMEM((tokens, width), BF16),
         bias=pltpu.VMEM((3, tokens, tokens), F32),
-        pick=pltpu.VMEM((slots, tokens), BF16),
+        pick=pltpu.VMEM((2, slots, tokens), BF16),
         place=pltpu.VMEM((2, tokens, slots), BF16),
         perm_f=pltpu.VMEM((slots, slots), BF16),
         perm_r=pltpu.VMEM((slots, slots), BF16),
-        g_send=chunked, g_z=chunked, g_mid=chunked, g_y=flat,
+        g_send=chunked, g_one=chunked, g_mid=chunked, g_two=chunked, g_in=flat,
         hid=pltpu.VMEM((groups, tokens, cols), BF16),
         h_send=chunked, h_z=chunked, h_mid=chunked, h_y=chunked,
         wg=weights, wu=weights, wd=weights,
@@ -81,7 +83,7 @@
 ):
     s = dict(zip(names, scratch))
     groups, tokens, cols = s["q"].shape
-    slots = s["pick"].shape[0]
+    slots = s["pick"].shape[1]
     width = groups * cols
     slice_cols = wd_hbm.shape[0]
     half = s["d_gate"].shape[2]
@@ -113,7 +115,7 @@
             steps.append(i)
             if count - i != i:
                 steps.append(count - i)
-        return steps
+        return steps[::-1]
 
     barrier = pltpu.get_barrier_semaphore()
     peers = [after, before, right, left, twin]
@@ -179,9 +181,9 @@
     dest_y = lax.shift_right_logical(expert, bits_zh + bits_zl)
     dest_z = (expert & (ZH - 1)) * ZL + (lax.shift_right_logical(expert, bits_zh) & (ZL - 1))
     target = jnp.where(rank < CAP, dest_z * z_rows + dest_y * CAP + rank, -1)
-    s["pick"][...] = onehot(jnp.broadcast_to(target, (slots, tokens)) == grid((slots, tokens), 0))
     target_y = jnp.where(rank < CAP, dest_y * y_rows + dest_z * CAP + rank, -1)
     for i, at in enumerate((target, target_y)):
+        s["pick"][i] = onehot(jnp.broadcast_to(at, (slots, tokens)) == grid((slots, tokens), 0))
         s["place"][i] = onehot(across(at) == grid((tokens, slots), 1).astype(F32))
 
     def regroup(index, outer, inner):
@@ -258,7 +260,7 @@
     for g in range(groups):
         at = pl.ds(g * cols, cols)
         rows = (weight_col * s["go"][:, at].astype(F32)).astype(BF16)
-        s["g_send"][g] = nn(s["pick"][...], rows).astype(BF16)
+        s["g_send"][g] = nn(s["pick"][1], rows).astype(BF16)
 
     wait(s["q"], s["load_q"])
     wait(s["kv"].at[0], s["load_kv"])
@@ -282,7 +284,7 @@
                 term = nn((raised[d] * share).astype(BF16), s["kv"][d, 1, g][:, at])
                 mixed = term if mixed is None else mixed + term
             s["hid"][g, :, at] = mixed.astype(BF16)
-        s["h_send"][g] = nn(s["pick"][...], s["hid"][g]).astype(BF16)
+        s["h_send"][g] = nn(s["pick"][0], s["hid"][g]).astype(BF16)
 
     @pl.loop(0, groups + 4)
     def _(step):
@@ -327,20 +329,28 @@
                 s["h_send"].at[g], s["h_z"].at[g], z_rows, zs, z, z_peer,
                 s["hz_s"].at[g], s["hz_r"].at[g],
             )
+
+        @pl.when((step >= G_START) & (step < groups + G_START))
+        def _():
+            g = step - G_START
             exchange(
-                s["g_send"].at[g], s["g_z"].at[g], z_rows, zs, z, z_peer,
+                s["g_send"].at[g], s["g_one"].at[g], y_rows, ys, y, y_peer,
+                s["gy_s"].at[g], s["gy_r"].at[g],
+            )
+
+        @pl.when((step >= G_LAG) & (step < groups + G_LAG))
+        def _():
+            g = step - G_LAG
+            wait(s["g_one"].at[g], s["gy_r"].at[g])
+            s["g_mid"][g] = nn(s["perm_r"][...], s["g_one"][g]).astype(BF16)
+            exchange(
+                s["g_mid"].at[g], s["g_two"].at[g], z_rows, zs, z, z_peer,
                 s["gz_s"].at[g], s["gz_r"].at[g],
             )
 
         @pl.when(step >= 4)
         def _():
             g = step - 4
-            wait(s["g_z"].at[g], s["gz_r"].at[g])
-            s["g_mid"][g] = nn(s["perm_f"][...], s["g_z"][g]).astype(BF16)
-            exchange(
-                s["g_mid"].at[g], s["g_y"].at[:, col(g)], y_rows, ys, y, y_peer,
-                s["gy_s"].at[g], s["gy_r"].at[g],
-            )
             wait(s["h_z"].at[g], s["hz_r"].at[g])
             s["h_mid"][g] = nn(s["perm_f"][...], s["h_z"][g]).astype(BF16)
             exchange(
@@ -374,7 +384,9 @@
         weights_in(a)
 
     for g in range(groups):
-        wait(s["g_y"].at[:, pl.ds(g * cols, cols)], s["gy_r"].at[g])
+        wait(s["g_two"].at[g], s["gz_r"].at[g])
+        at = pl.ds(g * cols, cols)
+        s["g_in"][:, at] = nn(s["perm_f"][...], s["g_two"][g]).astype(BF16)
     all_here(2)
 
     def units(part):
@@ -382,7 +394,7 @@
 
     @pl.loop(0, HALVES)
     def _(part):
-        s["d_act"][part] = nt(s["g_y"][...], s["wd"][units(part), :])
+        s["d_act"][part] = nt(s["g_in"][...], s["wd"][units(part), :])
 
     squares = None
     for g in range(groups):
@@ -465,8 +477,8 @@
         for hop in range(2):
             for part in range(2):
                 wait(s["kv"].at[hop, part, g], s["kv_s"].at[hop, part, g])
-        sent(s["g_send"].at[g], z_rows, zs, s["gz_s"].at[g])
-        sent(s["g_mid"].at[g], y_rows, ys, s["gy_s"].at[g])
+        sent(s["g_send"].at[g], y_rows, ys, s["gy_s"].at[g])
+        sent(s["g_mid"].at[g], z_rows, zs, s["gz_s"].at[g])
         sent(s["h_send"].at[g], z_rows, zs, s["hz_s"].at[g])
         sent(s["h_mid"].at[g], y_rows, ys, s["hy_s"].at[g])
 

time: 122 us -> 116 us (0.951)
  Pallas kernels: 120 us -> 114 us
    pallas_call x1, Pallas kernels: 120 us -> 114 us  [shards(): pl.pallas_call(functools.partial(kernel, tuple(scratch)), out_shape=jax.S...]
where the time goes in v4:
time: 116 us
  Pallas kernels  114 us (98%)
  local copies, waits for them, and re-layouts  1.88 us (2%)
    pallas_call x1, Pallas kernels, shards(): pl.pallas_call(functools.partial(kernel, tuple(scratch)), out_shape=jax.S...  114 us

profile of v4, /device:TPU:2, one launch (start us, length us, event | category | flops | bytes accessed | tf_op | source)
XLA Modules:
  0.0 116.2 jit_solution(10059372430443044755)
XLA Ops:
  0.0 114.3 %layer.1 = bf16[1,128,2048]{2,1,0:T(8,128)(2,1)} custom-call(s32[1,128]{1,0:T(1,128)} %doc_ref.1, s32[1,128]{1,0:T(1,128)} %bitcast.8, f32[1,128]{1,0:T(1,128)} %bitcast.9, f32[1,2048]{1,0:T(1,128)} %bitcast.7, bf16[1,128,2048]{2,1,0:T(8,128)(2,1)} %q_hbm.1, bf16[1,128,2048]{2,1,0:T(8,128)(2,1)} %k_hbm.1, bf16[1,128,2048]{2,1,0:T(8,128)(2,1)} %v_hbm.1, ...), custom_call_target="tpu_custom_call" | custom-call | tf_op jit(solution)/shard_map/layer/pallas_call | solution.py:505
  114.3 1.9 %copy.13 = bf16[1,128,2048]{2,1,0:T(8,128)(2,1)} copy(bf16[1,128,2048]{2,1,0:T(8,128)(2,1)} %layer.1) | data formatting | bytes 1048576
